TPU v7x, 32 devices: a whole 2x2x4 slice. The times are simulated.
32 devices in a mesh: replica: 2 (over x), shard: 16 (over z, y, core).
Axes of the slice: x: 2, y: 2, z: 4, core: 2. Of those that a mesh axis runs over, the one named last changes fastest.
Arguments:
- activations: bfloat16 [4096, 512], P(('replica', 'shard')), may hold values from -6 to 6
- cotangents: bfloat16 [4096, 8192], P(('replica', 'shard')), may hold values from -0.0078125 to 0.0078125
- statistics: float32 [2, 8192, 512], P(None, 'shard'), may hold values from -8 to 32, as said below
- roots: bfloat16 [2, 8192, 512], P(None, 'shard'), may hold values from -0.25 to 0.25
- ages: int32 [32], replicated, may hold values from 1 to 16
- refresh: int32 [32], replicated, may hold values 0 or 1
Outputs:
- update: bfloat16 [8192, 512], P('shard')
- new_statistics: float32 [2, 8192, 512], P(None, 'shard')
- new_roots: bfloat16 [2, 8192, 512], P(None, 'shard')
Inputs may be any that keep to these rules, and one draw needn't show every extreme that they name: `statistics`: for each block k, rows k * 512 to (k + 1) * 512 - 1 of either layer hold a symmetric positive definite 512 x 512 matrix.
All inputs are finite; a program needn't handle non-finite values.
Results may differ from a plain program's by a relative error of at most 0.0064.
Values may be sent and summed in bfloat16 or wider, within the bound.
A program may use at most 128 MiB of HBM per device.

v0:
```python
import math

import jax
import jax.numpy as jnp
from jax import lax
from jax.sharding import PartitionSpec as P

ITERS = 3


decay_base = 0.9
tiny_term = 1e-06


def from_partner(x, axis, apart):
    return lax.ppermute(x, axis, [(i, i ^ 1 << apart) for i in range(lax.axis_size(axis))])


def as_sent(x):
    return jax.tree.map(lambda a: a.astype(jnp.bfloat16) if a.dtype == jnp.float32 else a, x)


def newton(matrix):
    identity = jnp.eye(matrix.shape[-1], dtype=jnp.float32)
    frobenius = jnp.sqrt(jnp.sum(matrix * matrix) + tiny_term)
    scaling = 2.5 / frobenius
    iterate = scaling**0.25 * identity
    residual_map = scaling * matrix
    for sweep_index in range(ITERS):
        factor = (5.0 * identity - residual_map) * 0.25
        iterate = jnp.matmul(iterate, factor, precision=lax.Precision.HIGHEST)
        square = jnp.matmul(factor, factor, precision=lax.Precision.HIGHEST)
        fourth = jnp.matmul(square, square, precision=lax.Precision.HIGHEST)
        residual_map = jnp.matmul(fourth, residual_map, precision=lax.Precision.HIGHEST)
    return iterate


def gram_pair(blocks):
    left_gram = jnp.einsum("nij,nkj->nik", blocks, blocks, preferred_element_type=jnp.float32)
    right_gram = jnp.einsum("nji,njk->nik", blocks, blocks, preferred_element_type=jnp.float32)
    return jnp.stack([left_gram, right_gram], axis=1)


def stat_swap(values, bit_number):
    return from_partner(values, "shard", bit_number)


def block_swap(values, bit_number):
    return jax.tree.map(
        lambda part, own: part.astype(own.dtype),
        from_partner(as_sent(values), "shard", bit_number),
        values,
    )


def team_block(values, mover, team_size):
    shard_index = lax.axis_index("shard")
    gathered = values
    for bit_number in range(team_size.bit_length() - 1):
        partner = mover(gathered, bit_number)
        upper_side = jnp.right_shift(shard_index, bit_number) % 2 == 1
        below = jnp.concatenate([partner, gathered], axis=1)
        above = jnp.concatenate([gathered, partner], axis=1)
        gathered = jnp.where(upper_side, below, above)
    return gathered


def per_device(activations, cotangents, statistics, roots, ages, refresh):
    tokens_here = activations.shape[0]
    block_order = activations.shape[1]
    full_width = cotangents.shape[1]
    shards = lax.axis_size("shard")
    copies = lax.axis_size("replica")
    rows_here = statistics.shape[1]
    piece_rows = rows_here // copies
    reordered = (
        cotangents.reshape(tokens_here, shards, copies, piece_rows)
        .transpose(0, 2, 1, 3)
        .reshape(tokens_here, full_width)
    )
    total_piece = lax.psum_scatter(
        lax.dot_general(
            reordered, activations, (((0,), (0,)), ((), ())), preferred_element_type=jnp.float32
        ),
        ("replica", "shard"),
        scatter_dimension=0,
        tiled=True,
    )
    gradient = lax.all_gather(total_piece.astype(jnp.bfloat16), "replica", axis=0, tiled=True)
    shard_index = lax.axis_index("shard")
    if rows_here < block_order:
        team_size = block_order // rows_here
        team_place = shard_index % team_size
        first_block = shard_index // team_size
        row_start = team_place * rows_here
        blocks_here = 1
        old_stats = team_block(statistics, stat_swap, team_size)[:, None]
        full_pair = team_block(jnp.stack([gradient, roots[1]]), block_swap, team_size)
        grad_blocks = full_pair[0][None]
        right_old = full_pair[1][None]

        def own_rows(blocks):
            return lax.dynamic_slice_in_dim(blocks[0], row_start, rows_here, 0)

    else:
        blocks_here = rows_here // block_order
        first_block = shard_index * blocks_here
        old_stats = statistics.reshape(2, blocks_here, block_order, block_order)
        grad_blocks = gradient.reshape(blocks_here, block_order, block_order)
        right_old = roots[1].reshape(blocks_here, block_order, block_order)

        def own_rows(blocks):
            return blocks.reshape(rows_here, blocks.shape[-1])

    count_here = 2 * blocks_here
    gram_pairs = gram_pair(grad_blocks).reshape(count_here, block_order, block_order)
    previous = old_stats.transpose(1, 0, 2, 3).reshape(count_here, block_order, block_order)
    ages_here = lax.dynamic_slice_in_dim(ages, 2 * first_block, count_here, 0)
    fresh_here = lax.dynamic_slice_in_dim(refresh, 2 * first_block, count_here, 0) == 1
    decay_factor = (decay_base ** ages_here.astype(jnp.float32))[:, None, None]
    updated = jnp.where(
        fresh_here[:, None, None],
        decay_factor * previous + (1.0 - decay_factor) * gram_pairs,
        previous,
    )
    refreshed = jax.vmap(newton)(updated).astype(jnp.bfloat16)
    root_pairs = refreshed.reshape(blocks_here, 2, block_order, block_order)
    fresh_pairs = fresh_here.reshape(blocks_here, 2)
    right_full = jnp.where(fresh_pairs[:, 1, None, None], root_pairs[:, 1], right_old)
    left_mask = own_rows(
        jnp.broadcast_to(fresh_pairs[:, 0, None, None], (blocks_here, block_order, 1))
    )
    left_rows = jnp.where(left_mask, own_rows(root_pairs[:, 0]), roots[0])
    new_roots = jnp.stack([left_rows, own_rows(right_full)])
    stat_pairs = updated.reshape(blocks_here, 2, block_order, block_order)
    new_statistics = jnp.stack([own_rows(stat_pairs[:, 0]), own_rows(stat_pairs[:, 1])])
    mixed_blocks = jnp.einsum(
        "nij,njk->nik", grad_blocks, right_full, preferred_element_type=jnp.float32
    ).astype(jnp.bfloat16)
    left_blocks = left_rows.reshape(blocks_here, -1, block_order)
    product = jnp.einsum(
        "nij,njk->nik", left_blocks, mixed_blocks, preferred_element_type=jnp.float32
    )
    update = (product.reshape(rows_here, block_order) * math.sqrt(block_order)).astype(jnp.bfloat16)
    return (update, new_statistics, new_roots)


def solution(mesh):
    in_specs = (
        P(("replica", "shard"), None),
        P(("replica", "shard"), None),
        P(None, "shard", None),
        P(None, "shard", None),
        P(),
        P(),
    )
    out_specs = (P("shard", None), P(None, "shard", None), P(None, "shard", None))
    return jax.shard_map(
        per_device, mesh=mesh, in_specs=in_specs, out_specs=out_specs, check_vma=False
    )
```

profile of v0, /device:TPU:0, one launch (start us, length us, event | category | flops | bytes accessed | tf_op | source)
XLA Modules:
  0.0 267.5 jit_solution(3113053441379582157)
XLA Ops:
  7.2 0.0 reduce-scatter.2.cloned.1.call-start
  7.2 3.2 %copy.9 = bf16[128,8192]{0,1:T(8,128)(2,1)S(1)} copy(bf16[128,8192]{1,0:T(8,128)(2,1)} %param.7) | data formatting | bytes 4194304 | tf_op args[1]
  10.5 0.2 copy.10
  10.7 8.1 %fusion.49 = f32[8192,512]{1,0:T(8,128)} fusion(bf16[128,8192]{0,1:T(8,128)(2,1)S(1)} %bitcast.60, bf16[128,512]{1,0:T(8,128)(2,1)S(1)} %copy-done), kind=kOutput, calls=%fused_computation.63 | convolution fusion | flops 1073741824 | bytes 19005440 | tf_op jit(solution)/shard_map/dot_general | solution.py:82
  18.8 0.6 copy-done.7
  19.4 0.1 dynamic-slice_compare_fusion
  19.5 0.1 fusion.69
  19.6 0.1 broadcast_subtract_fusion
  19.7 0.6 fusion.48
  20.3 0.1 fusion.34
  20.4 1.1 fusion.35
  21.5 184.7 %reduce-scatter.2.cloned.1.call-done = f32[256,512]{1,0:T(8,128)} async-done(((f32[8192,512]{1,0:T(8,128)}), f32[256,512]{1,0:T(8,128)}) %reduce-scatter.2.cloned.1.call-update) | async-done | bytes 524304 | tf_op jit(solution)/shard_map/reduce_scatter | solution.py:81
  206.2 1.1 convert_element_type.24
  207.3 8.3 %all_gather.3 = bf16[512,512]{1,0:T(8,128)(2,1)S(1)} all-gather(bf16[256,512]{1,0:T(8,128)(2,1)S(1)} %convert_element_type.24), channel_id=1, replica_groups=mesh['replica'=2,'shard'=16] {'replica'}, dimensions={0}, use_global_device_ids=true | all-gather | bytes 786432 | tf_op jit(solution)/shard_map/all_gather | solution.py:89
  215.6 0.5 convolution_bitcast_fusion
  216.1 0.5 convolution_bitcast_fusion.1
  216.5 0.8 copy-done.4
  217.4 0.9 multiply_reduce_fusion
  218.2 4.0 %fusion.12 = f32[2,512,512]{2,1,0:T(8,128)S(1)} fusion(f32[2,512,512]{2,1,0:T(8,128)S(1)} %get-tuple-element.4, f32[2]{0:T(128)S(1)} %get-tuple-element.14, f32[512,512]{1,0:T(8,128)S(1)} %fusion.34), kind=kOutput, calls=%fused_computation.17 | convolution fusion | flops 3222798336 | bytes 5242888 | tf_op jit(solution)/shard_map/vmap()/dot_general | solution.py:32
  222.2 3.5 %fusion.50 = f32[2,512,512]{2,1,0:T(8,128)S(1)} fusion(f32[2,512,512]{2,1,0:T(8,128)S(1)} %fusion.12), kind=kOutput, calls=%fused_computation.64 | convolution fusion | flops 3221225472 | bytes 4194304 | tf_op jit(solution)/shard_map/vmap()/dot_general | solution.py:33
  225.8 3.7 %fusion.8 = f32[2,512,512]{2,1,0:T(8,128)S(1)} fusion(f32[2,512,512]{2,1,0:T(8,128)S(1)} %fusion.50, f32[2,512,512]{2,1,0:T(8,128)S(1)} %get-tuple-element.4, f32[2]{0:T(128)S(1)} %get-tuple-element.14), kind=kOutput, calls=%fused_computation.13 | convolution fusion | flops 3221749760 | bytes 6291464 | tf_op jit(solution)/shard_map/vmap()/dot_general | solution.py:34
  229.5 4.0 %fusion.10 = f32[2,512,512]{2,1,0:T(8,128)S(1)} fusion(f32[2,512,512]{2,1,0:T(8,128)S(1)} %fusion.8, f32[512,512]{1,0:T(8,128)S(1)} %fusion.34), kind=kOutput, calls=%fused_computation.15 | convolution fusion | flops 3222274048 | bytes 5242880 | tf_op jit(solution)/shard_map/vmap()/dot_general | solution.py:32
  233.5 3.9 %fusion.6 = f32[2,512,512]{2,1,0:T(8,128)S(1)} fusion(f32[2,512,512]{2,1,0:T(8,128)S(1)} %get-tuple-element.4, f32[2]{0:T(128)S(1)} %get-tuple-element.14, f32[512,512]{1,0:T(8,128)S(1)} %fusion.34, f32[512,512]{1,0:T(8,128)S(1)} %copy-done.3, f32[2]{0:T(128)S(1)} %get-tuple-element.13), kind=kOutput, calls=%fused_computation.10 | convolution fusion | flops 3223322624 | bytes 6291472 | tf_op jit(solution)/shard_map/vmap()/dot_general | solution.py:31
  237.4 3.7 %fusion.11 = f32[2,512,512]{2,1,0:T(8,128)S(1)} fusion(f32[2,512,512]{2,1,0:T(8,128)S(1)} %fusion.6, f32[2,512,512]{2,1,0:T(8,128)S(1)} %fusion.8, f32[512,512]{1,0:T(8,128)S(1)} %fusion.34), kind=kOutput, calls=%fused_computation.16 | convolution fusion | flops 3222274048 | bytes 7340032 | tf_op jit(solution)/shard_map/vmap()/dot_general | solution.py:31
  241.0 3.8 %fusion.51 = f32[2,512,512]{2,1,0:T(8,128)S(1)} fusion(f32[2,512,512]{2,1,0:T(8,128)S(1)} %fusion.10), kind=kOutput, calls=%fused_computation.65 | convolution fusion | flops 3221225472 | bytes 4194304 | tf_op jit(solution)/shard_map/vmap()/dot_general | solution.py:33
  244.8 3.5 %fusion.52 = f32[2,512,512]{2,1,0:T(8,128)S(1)} fusion(f32[2,512,512]{2,1,0:T(8,128)S(1)} %fusion.51, f32[2,512,512]{2,1,0:T(8,128)S(1)} %fusion.8), kind=kOutput, calls=%fused_computation.66 | convolution fusion | flops 3221225472 | bytes 6291456 | tf_op jit(solution)/shard_map/vmap()/dot_general | solution.py:34
  248.4 3.7 %fusion.16 = bf16[1,2,512,512]{3,2,1,0:T(8,128)(2,1)S(1)} fusion(f32[2,512,512]{2,1,0:T(8,128)S(1)} %fusion.11, f32[2,512,512]{2,1,0:T(8,128)S(1)} %fusion.52, f32[512,512]{1,0:T(8,128)S(1)} %fusion.34), kind=kOutput, calls=%fused_computation.19 | convolution fusion | flops 3222798336 | bytes 6291456 | tf_op jit(solution)/shard_map/vmap()/dot_general | solution.py:31
  252.1 2.2 fusion.38
  254.3 2.6 fusion.19
  256.9 2.1 pad_maximum_fusion.1
  259.0 0.2 slice_bitcast_fusion.1
  259.2 1.5 pad_maximum_fusion
  (16 shorter events, 0.1 us)
Async XLA Ops:
  7.2 3.5 %copy-start = (bf16[128,512]{1,0:T(8,128)(2,1)S(1)}, bf16[128,512]{1,0:T(8,128)(2,1)}, u32[]{:S(2)}) copy-start(bf16[128,512]{1,0:T(8,128)(2,1)} %param.6) | copy-start | bytes 393220
  7.2 199.0 %reduce-scatter.2.cloned.1.call-start = ((), (), s32[]{:S(2)}) async-start(), calls=%async_computation.1 | async-start | bytes 17301504 | tf_op jit(solution)/shard_map/reduce_scatter | solution.py:81
  18.8 0.7 copy-start.7
  18.8 0.8 copy-start.6
  215.6 0.9 copy-start.1
  215.6 1.8 copy-start.4
  229.5 4.0 %copy-start.3 = (f32[512,512]{1,0:T(8,128)S(1)}, f32[512,512]{1,0:T(8,128)}, u32[]{:S(2)}) copy-start(f32[512,512]{1,0:T(8,128)} %fusion.35) | copy-start | bytes 3145732
  248.4 3.7 %copy-start.5 = (bf16[2,512,512]{2,1,0:T(8,128)(2,1)S(1)}, bf16[2,512,512]{2,1,0:T(8,128)(2,1)}, u32[]{:S(2)}) copy-start(bf16[2,512,512]{2,1,0:T(8,128)(2,1)} %param.9) | copy-start | bytes 3145732
  252.1 2.2 copy-start.2
Sparse Core Ops, SparseCore 0:
  18.9 187.2 reduce-scatter.1
where the time goes:
time: 268 us; the launch traced here: 267 us
  waiting for transfers between devices  185 us (69%)
  matrix products  45.3 us (17%)
  between operations  14.2 us (5%)
  other arithmetic  9.17 us (3%)
  blocking collectives  8.32 us (3%)
  local copies, waits for them, and re-layouts  5.72 us (2%)
    reduce_scatter x1, waiting for transfers between devices, per_device(): lax.psum_scatter(lax.dot_general(reordered, activations, (((0,), (0,)), (...  185 us
    dot_general x3, matrix products, newton(): iterate = jnp.matmul(iterate, factor, precision=lax.Precision.HIGHEST)  11.2 us
    all_gather x1, blocking collectives, per_device(): lax.all_gather(total_piece.astype(jnp.bfloat16), 'replica', axis=0, tiled...  8.32 us
    dot_general x1, matrix products, per_device(): lax.dot_general(reordered, activations, (((0,), (0,)), ((), ())), preferr...  8.08 us
    dot_general x2, matrix products, newton(): square = jnp.matmul(factor, factor, precision=lax.Precision.HIGHEST)  7.94 us
    dot_general x2, matrix products, newton(): fourth = jnp.matmul(square, square, precision=lax.Precision.HIGHEST)  7.33 us
    dot_general x2, matrix products, newton(): jnp.matmul(fourth, residual_map, precision=lax.Precision.HIGHEST)  7.21 us
  transfers between devices with their start and end apart: 1, of which 1 were waited for; matrix products, arithmetic and copies ran while one was open for 1% of the time, Pallas kernels for 0%

commit v1 on v0

--- a/solution.py
+++ b/solution.py
@@ -1,8 +1,11 @@
+import functools
 import math
 
 import jax
 import jax.numpy as jnp
 from jax import lax
+from jax.experimental import pallas as pl
+from jax.experimental.pallas import tpu as pltpu
 from jax.sharding import PartitionSpec as P
 
 ITERS = 3
@@ -65,7 +68,7 @@
     return gathered
 
 
-def per_device(activations, cotangents, statistics, roots, ages, refresh):
+def general(activations, cotangents, statistics, roots, ages, refresh):
     tokens_here = activations.shape[0]
     block_order = activations.shape[1]
     full_width = cotangents.shape[1]
@@ -145,6 +148,270 @@
     return (update, new_statistics, new_roots)
 
 
+CORES = 2
+LANES = 2
+MESH = pl.DeviceIdType.MESH
+
+
+def exchange_kernel(
+    sizes, cot_ref, act_ref, grad_ref, cots, acts, outgoing, incoming, grad,
+    local_sem, act_send, act_recv, relay_send, cot_send, cot_recv,
+    part_send, part_recv, grad_send, grad_recv,
+):
+    copies, levels, block, tokens, rows = sizes
+    piece = rows // copies
+    team = CORES * LANES
+    here = lax.axis_index("replica")
+    shard = lax.axis_index("shard")
+    level = shard // team
+    lane = (shard // CORES) % LANES
+    core = shard % CORES
+    slots = [(a, b, c) for a in range(copies) for b in range(LANES) for c in range(CORES)]
+
+    def peer(offset):
+        a, b, c = offset
+        other = (level * LANES + (lane + b) % LANES) * CORES + (core + c) % CORES
+        return ((here + a) % copies, other)
+
+    def level_peer(step):
+        return (here, ((level + step) % levels) * team + lane * CORES + core)
+
+    def columns(device, step):
+        target = ((level + step) % levels) * team + device[1] % team
+        return pl.ds(pl.multiple_of(target * rows + device[0] * piece, piece), piece)
+
+    barrier = pltpu.get_barrier_semaphore()
+    for offset in slots[1:]:
+        pl.semaphore_signal(barrier, inc=1, device_id=peer(offset), device_id_type=MESH)
+    for step in range(1, levels):
+        pl.semaphore_signal(barrier, inc=1, device_id=level_peer(step), device_id_type=MESH)
+    own_act = pltpu.make_async_copy(act_ref, acts.at[pl.ds(0, tokens)], local_sem.at[0])
+    own_act.start()
+    own_cots = []
+    for k in range(levels):
+        own = pltpu.make_async_copy(
+            cot_ref.at[:, columns((here, shard), k + 1)],
+            cots.at[k, pl.ds(0, tokens)],
+            local_sem.at[1 + k],
+        )
+        own.start()
+        own_cots.append(own)
+    pl.semaphore_wait(barrier, len(slots) - 1 + levels - 1)
+
+    sends = []
+    act_in = {}
+    for index, offset in enumerate(slots):
+        if index == 0:
+            continue
+        direct = offset[2] == 0 or offset == (0, 0, 1)
+        copy = pltpu.make_async_remote_copy(
+            src_ref=act_ref,
+            dst_ref=acts.at[pl.ds(index * tokens, tokens)],
+            send_sem=act_send.at[index],
+            recv_sem=act_recv.at[index],
+            device_id=peer(offset),
+            device_id_type=MESH,
+        )
+        act_in[index] = copy
+        if direct:
+            copy.start()
+            sends.append(copy)
+    cot_in = {}
+    for k in range(levels):
+        for index, offset in enumerate(slots):
+            if index == 0:
+                continue
+            device = peer(offset)
+            copy = pltpu.make_async_remote_copy(
+                src_ref=cot_ref.at[:, columns(device, k + 1)],
+                dst_ref=cots.at[k, pl.ds(index * tokens, tokens)],
+                send_sem=cot_send.at[k, index],
+                recv_sem=cot_recv.at[k, index],
+                device_id=device,
+                device_id_type=MESH,
+            )
+            copy.start()
+            sends.append(copy)
+            cot_in[k, index] = copy
+    for index, offset in enumerate(slots):
+        if index == 0 or offset[2] != 0:
+            continue
+        act_in[index].wait_recv()
+        relay = pltpu.make_async_remote_copy(
+            src_ref=acts.at[pl.ds(index * tokens, tokens)],
+            dst_ref=acts.at[pl.ds((index + 1) * tokens, tokens)],
+            send_sem=relay_send.at[index],
+            recv_sem=act_recv.at[index + 1],
+            device_id=peer((0, 0, 1)),
+            device_id_type=MESH,
+        )
+        relay.start()
+        sends.append(relay)
+    own_act.wait()
+    for index, offset in enumerate(slots):
+        if offset[2] != 0:
+            act_in[index].wait_recv()
+
+    parts = []
+    for k in range(levels):
+        own_cots[k].wait()
+        for index in range(1, len(slots)):
+            cot_in[k, index].wait_recv()
+        part = lax.dot_general(
+            cots[k], acts[...], (((0,), (0,)), ((), ())), preferred_element_type=jnp.float32
+        )
+        if k < levels - 1:
+            outgoing[k] = part.astype(jnp.bfloat16)
+            copy = pltpu.make_async_remote_copy(
+                src_ref=outgoing.at[k],
+                dst_ref=incoming.at[k],
+                send_sem=part_send.at[k],
+                recv_sem=part_recv.at[k],
+                device_id=level_peer(k + 1),
+                device_id_type=MESH,
+            )
+            copy.start()
+            parts.append(copy)
+    total = part
+    for k in range(levels - 1):
+        parts[k].wait_recv()
+        total += incoming[k].astype(jnp.float32)
+    mine = pl.ds(pl.multiple_of(here * piece, piece), piece)
+    grad[mine] = total.astype(jnp.bfloat16)
+    finals = []
+    for step in range(1, copies):
+        copy = pltpu.make_async_remote_copy(
+            src_ref=grad.at[mine],
+            dst_ref=grad.at[mine],
+            send_sem=grad_send.at[step],
+            recv_sem=grad_recv.at[step],
+            device_id=((here + step) % copies, shard),
+            device_id_type=MESH,
+        )
+        copy.start()
+        finals.append(copy)
+    for copy in sends + parts:
+        copy.wait_send()
+    for copy in finals:
+        copy.wait()
+    grad_ref[...] = grad[...]
+
+
+def exchange(cotangents, activations, copies, levels, rows):
+    tokens, block = activations.shape
+    team = CORES * LANES
+    many = copies * team
+    piece = rows // copies
+    dma = pltpu.SemaphoreType.DMA
+    return pl.pallas_call(
+        functools.partial(exchange_kernel, (copies, levels, block, tokens, rows)),
+        out_shape=jax.ShapeDtypeStruct((rows, block), jnp.bfloat16),
+        in_specs=[pl.BlockSpec(memory_space=pl.ANY), pl.BlockSpec(memory_space=pl.ANY)],
+        out_specs=pl.BlockSpec(memory_space=pltpu.VMEM),
+        scratch_shapes=[
+            pltpu.VMEM((levels, many * tokens, piece), jnp.bfloat16),
+            pltpu.VMEM((many * tokens, block), jnp.bfloat16),
+            pltpu.VMEM((levels, piece, block), jnp.bfloat16),
+            pltpu.VMEM((levels, piece, block), jnp.bfloat16),
+            pltpu.VMEM((rows, block), jnp.bfloat16),
+            dma((1 + levels,)),
+            dma((many,)),
+            dma((many,)),
+            dma((many,)),
+            dma((levels, many)),
+            dma((levels, many)),
+            dma((levels,)),
+            dma((levels,)),
+            dma((copies,)),
+            dma((copies,)),
+        ],
+        compiler_params=pltpu.CompilerParams(collective_id=0, has_side_effects=True),
+        name="exchange",
+    )(cotangents, activations)
+
+
+def product(left, right, contract=((1,), (0,))):
+    return lax.dot_general(left, right, (contract, ((), ())), preferred_element_type=jnp.float32)
+
+
+def small(x):
+    return x.astype(jnp.bfloat16)
+
+
+def root_step(n):
+    half = small(n)
+    q = product(half, half) - 2.5 * n
+    half_q = small(q)
+    r = product(half_q, half_q) + 3.125 * q
+    return product(small(r), half) + 1.25**4 * n
+
+
+def refresh_kernel(grad_ref, stats_ref, roots_ref, ages_ref, fresh_ref,
+                   update_ref, new_stats_ref, new_roots_ref):
+    first = 2 * lax.axis_index("shard")
+    block = grad_ref.shape[0]
+    grad = grad_ref[...]
+    grams = [lambda: product(grad, grad, ((1,), (1,))), lambda: product(grad, grad, ((0,), (0,)))]
+    maps, scales, fresh = [], [], []
+    for side in range(2):
+        is_fresh = fresh_ref[first + side] == 1
+        age = jnp.full((1, 1), ages_ref[first + side].astype(jnp.float32), jnp.float32)
+        decay = jnp.exp(age * math.log(decay_base))
+        old = stats_ref[side]
+        new = jnp.where(is_fresh, decay * old + (1.0 - decay) * grams[side](), old)
+        new_stats_ref[side] = new
+        total = jnp.sum(jnp.sum(new * new, axis=0, keepdims=True), axis=1, keepdims=True)
+        scaling = 2.5 / jnp.sqrt(total + tiny_term)
+        maps.append((0.25 * scaling) * new)
+        scales.append(jnp.sqrt(jnp.sqrt(scaling)))
+        fresh.append(is_fresh)
+    n1 = maps
+    n2 = [root_step(n) for n in n1]
+    x2 = [product(small(a), small(b)) - 1.25 * (a + b) for a, b in zip(n1, n2)]
+    n3 = [root_step(n) for n in n2]
+    row = lax.broadcasted_iota(jnp.int32, (block, block), 0)
+    column = lax.broadcasted_iota(jnp.int32, (block, block), 1)
+    diagonal = jnp.where(row == column, 1.25**3, 0.0)
+    roots = []
+    for side in range(2):
+        last = diagonal + 1.25 * x2[side] - 1.5625 * n3[side]
+        last = last - product(small(x2[side]), small(n3[side]))
+        root = small(scales[side] * last)
+        root = jnp.where(fresh[side], root, roots_ref[side])
+        new_roots_ref[side] = root
+        roots.append(root)
+    mixed = small(product(grad, roots[1]))
+    update_ref[...] = small(product(roots[0], mixed) * math.sqrt(block))
+
+
+def refresh_roots(gradient, statistics, roots, ages, refresh):
+    vmem = pl.BlockSpec(memory_space=pltpu.VMEM)
+    smem = pl.BlockSpec(memory_space=pltpu.SMEM)
+    return pl.pallas_call(
+        refresh_kernel,
+        out_shape=(
+            jax.ShapeDtypeStruct(gradient.shape, jnp.bfloat16),
+            jax.ShapeDtypeStruct(statistics.shape, jnp.float32),
+            jax.ShapeDtypeStruct(roots.shape, jnp.bfloat16),
+        ),
+        in_specs=[vmem, vmem, vmem, smem, smem],
+        out_specs=(vmem, vmem, vmem),
+        name="refresh_roots",
+    )(gradient, statistics, roots, ages, refresh)
+
+
+def per_device(activations, cotangents, statistics, roots, ages, refresh):
+    shards = lax.axis_size("shard")
+    copies = lax.axis_size("replica")
+    rows = statistics.shape[1]
+    block = activations.shape[1]
+    team = CORES * LANES
+    if rows != block or shards % team or rows % copies or (rows // copies) % 128:
+        return general(activations, cotangents, statistics, roots, ages, refresh)
+    gradient = exchange(cotangents, activations, copies, shards // team, rows)
+    return refresh_roots(gradient, statistics, roots, ages, refresh)
+
+
 def solution(mesh):
     in_specs = (
         P(("replica", "shard"), None),

time: 268 us -> 63.3 us (0.24)
  waiting for transfers between devices: 185 us -> 0 us
  Pallas kernels: 0 us -> 62.5 us
  matrix products: 45.3 us -> 0 us
  between operations: 14.2 us -> 0.64 us
  other arithmetic: 9.17 us -> 0 us
  blocking collectives: 8.32 us -> 0 us
  local copies, waits for them, and re-layouts: 5.72 us -> 0 us
    reduce_scatter x1 -> x0, waiting for transfers between devices: 185 us -> none  [per_device(): lax.psum_scatter(lax.dot_general(reordered, activations, (((0,), (0,)), (...]
    pallas_call x0 -> x2, Pallas kernels: none -> 62.5 us  [the longest x1 52.8 us: exchange(): pl.pallas_call(functools.partial(exchange_kernel, (copies, levels, block,...]
    dot_general x13 -> x0, matrix products: 45.3 us -> none  [the longest x3 11.2 us: newton(): iterate = jnp.matmul(iterate, factor, precision=lax.Precision.HIGHEST)]
    all_gather x1 -> x0, blocking collectives: 8.32 us -> none  [per_device(): lax.all_gather(total_piece.astype(jnp.bfloat16), 'replica', axis=0, tiled...]
    unnamed x17 -> x0, local copies, waits for them, and re-layouts: 4.72 us -> none
    another operation x2 -> x0, other arithmetic: 3.6 us -> none  [the longest x1 2.11 us: per_device(): new_roots = jnp.stack([left_rows, own_rows(right_full)])]
  transfers between devices with their start and end apart: 1 -> 0, of which waited for: 1 -> 0; matrix products, arithmetic and copies ran while one was open for 1% -> 0% of each run, Pallas kernels for 0% -> 0%
where the time goes in v1:
time: 63.3 us; the launch traced here: 63.2 us
  Pallas kernels  62.5 us (99%)
  between operations  0.64 us (1%)
    pallas_call x1, Pallas kernels, exchange(): pl.pallas_call(functools.partial(exchange_kernel, (copies, levels, block,...  52.8 us
    pallas_call x1, Pallas kernels, refresh_roots(): pl.pallas_call(refresh_kernel, out_shape=(jax.ShapeDtypeStruct(gradient.s...  9.68 us

profile of v1, /device:TPU:0, one launch (start us, length us, event | category | flops | bytes accessed | tf_op | source)
XLA Modules:
  0.0 63.2 jit_solution(1740924907445724484)
XLA Ops:
  0.6 52.8 %exchange.1.grad_ref = bf16[512,512]{1,0:T(8,128)(2,1)} custom-call(bf16[128,8192]{1,0:T(8,128)(2,1)} %cot_ref.1, bf16[128,512]{1,0:T(8,128)(2,1)} %act_ref.1), custom_call_target="tpu_custom_call" | custom-call | tf_op jit(solution)/shard_map/exchange/pallas_call | solution.py:306
  53.5 9.7 %refresh_roots.1 = (bf16[512,512]{1,0:T(8,128)(2,1)}, f32[2,512,512]{2,1,0:T(8,128)}, bf16[2,512,512]{2,1,0:T(8,128)(2,1)}) custom-call(bf16[512,512]{1,0:T(8,128)(2,1)} %exchange.1.grad_ref, f32[2,512,512]{2,1,0:T(8,128)} %stats_ref.1, bf16[2,512,512]{2,1,0:T(8,128)(2,1)} %roots_ref.1, s32[32]{0:T(128)} %ages_ref.1, s32[32]{0:T(128)} %fresh_ref.1), custom_call_target="tpu_custom_call" | custom-call | tf_op jit(solution)/shard_map/refresh_roots/pallas_call | solution.py:390

commit v2 on v1

--- a/solution.py
+++ b/solution.py
@@ -150,6 +150,8 @@
 
 CORES = 2
 LANES = 2
+SPLIT = 2
+VMEM = 24 << 20
 MESH = pl.DeviceIdType.MESH
 
 
@@ -158,8 +160,9 @@
     local_sem, act_send, act_recv, relay_send, cot_send, cot_recv,
     part_send, part_recv, grad_send, grad_recv,
 ):
-    copies, levels, block, tokens, rows = sizes
+    copies, levels, tokens, rows = sizes
     piece = rows // copies
+    part_rows = piece // SPLIT
     team = CORES * LANES
     here = lax.axis_index("replica")
     shard = lax.axis_index("shard")
@@ -167,6 +170,7 @@
     lane = (shard // CORES) % LANES
     core = shard % CORES
     slots = [(a, b, c) for a in range(copies) for b in range(LANES) for c in range(CORES)]
+    steps = [(part, k) for part in range(SPLIT) for k in range(levels)]
 
     def peer(offset):
         a, b, c = offset
@@ -176,121 +180,132 @@
     def level_peer(step):
         return (here, ((level + step) % levels) * team + lane * CORES + core)
 
-    def columns(device, step):
-        target = ((level + step) % levels) * team + device[1] % team
-        return pl.ds(pl.multiple_of(target * rows + device[0] * piece, piece), piece)
+    def columns(device, part, k):
+        target = ((level + k + 1) % levels) * team + device[1] % team
+        start = target * rows + device[0] * piece + part * part_rows
+        return pl.ds(pl.multiple_of(start, part_rows), part_rows)
+
+    def token_rows(index):
+        return pl.ds(index * tokens, tokens)
 
     barrier = pltpu.get_barrier_semaphore()
     for offset in slots[1:]:
         pl.semaphore_signal(barrier, inc=1, device_id=peer(offset), device_id_type=MESH)
     for step in range(1, levels):
         pl.semaphore_signal(barrier, inc=1, device_id=level_peer(step), device_id_type=MESH)
-    own_act = pltpu.make_async_copy(act_ref, acts.at[pl.ds(0, tokens)], local_sem.at[0])
+    own_act = pltpu.make_async_copy(act_ref, acts.at[token_rows(0)], local_sem.at[0])
     own_act.start()
     own_cots = []
-    for k in range(levels):
+    for turn, (part, k) in enumerate(steps):
         own = pltpu.make_async_copy(
-            cot_ref.at[:, columns((here, shard), k + 1)],
-            cots.at[k, pl.ds(0, tokens)],
-            local_sem.at[1 + k],
+            cot_ref.at[:, columns((here, shard), part, k)],
+            cots.at[turn, token_rows(0)],
+            local_sem.at[1 + turn],
         )
         own.start()
         own_cots.append(own)
     pl.semaphore_wait(barrier, len(slots) - 1 + levels - 1)
 
     sends = []
-    act_in = {}
-    for index, offset in enumerate(slots):
-        if index == 0:
-            continue
-        direct = offset[2] == 0 or offset == (0, 0, 1)
+
+    def send_act(offset, direct, via):
+        index = slots.index(offset)
+        first = slots.index(tuple(o - v for o, v in zip(offset, via)))
         copy = pltpu.make_async_remote_copy(
-            src_ref=act_ref,
-            dst_ref=acts.at[pl.ds(index * tokens, tokens)],
+            src_ref=act_ref if direct else acts.at[token_rows(first)],
+            dst_ref=acts.at[token_rows(index)],
             send_sem=act_send.at[index],
             recv_sem=act_recv.at[index],
-            device_id=peer(offset),
+            device_id=peer(via),
             device_id_type=MESH,
         )
-        act_in[index] = copy
-        if direct:
-            copy.start()
-            sends.append(copy)
+        copy.start()
+        sends.append(copy)
+        return copy
+
     cot_in = {}
-    for k in range(levels):
-        for index, offset in enumerate(slots):
-            if index == 0:
-                continue
-            device = peer(offset)
+
+    def send_cots(turns):
+        for turn in turns:
+            for index in range(1, len(slots)):
+                device = peer(slots[index])
+                copy = pltpu.make_async_remote_copy(
+                    src_ref=cot_ref.at[:, columns(device, *steps[turn])],
+                    dst_ref=cots.at[turn, token_rows(index)],
+                    send_sem=cot_send.at[turn, index],
+                    recv_sem=cot_recv.at[turn, index],
+                    device_id=device,
+                    device_id_type=MESH,
+                )
+                copy.start()
+                sends.append(copy)
+                cot_in[turn, index] = copy
+
+    act_in = {}
+    for a in range(1, copies):
+        act_in[a, 0, 0] = send_act((a, 0, 0), True, (a, 0, 0))
+    for b in range(1, LANES):
+        act_in[0, b, 0] = send_act((0, b, 0), True, (0, b, 0))
+    for c in range(1, CORES):
+        act_in[0, 0, c] = send_act((0, 0, c), True, (0, 0, c))
+    send_cots(range(1))
+    for a in range(1, copies):
+        act_in[a, 0, 0].wait_recv()
+        for b in range(1, LANES):
+            act_in[a, b, 0] = send_act((a, b, 0), False, (0, b, 0))
+    send_cots(range(1, len(steps)))
+    for a in range(copies):
+        for b in range(LANES):
+            if b:
+                act_in[a, b, 0].wait_recv()
+            if a or b:
+                for c in range(1, CORES):
+                    act_in[a, b, c] = send_act((a, b, c), False, (0, 0, c))
+    own_act.wait()
+    for offset in slots:
+        if offset[2]:
+            act_in[offset].wait_recv()
+
+    parts, finals = {}, []
+    for turn, (part, k) in enumerate(steps):
+        own_cots[turn].wait()
+        for index in range(1, len(slots)):
+            cot_in[turn, index].wait_recv()
+        term = lax.dot_general(
+            cots[turn], acts[...], (((0,), (0,)), ((), ())), preferred_element_type=jnp.float32
+        )
+        if k < levels - 1:
+            outgoing[turn] = term.astype(jnp.bfloat16)
             copy = pltpu.make_async_remote_copy(
-                src_ref=cot_ref.at[:, columns(device, k + 1)],
-                dst_ref=cots.at[k, pl.ds(index * tokens, tokens)],
-                send_sem=cot_send.at[k, index],
-                recv_sem=cot_recv.at[k, index],
-                device_id=device,
+                src_ref=outgoing.at[turn],
+                dst_ref=incoming.at[turn],
+                send_sem=part_send.at[turn],
+                recv_sem=part_recv.at[turn],
+                device_id=level_peer(k + 1),
                 device_id_type=MESH,
             )
             copy.start()
             sends.append(copy)
-            cot_in[k, index] = copy
-    for index, offset in enumerate(slots):
-        if index == 0 or offset[2] != 0:
+            parts[turn] = copy
             continue
-        act_in[index].wait_recv()
-        relay = pltpu.make_async_remote_copy(
-            src_ref=acts.at[pl.ds(index * tokens, tokens)],
-            dst_ref=acts.at[pl.ds((index + 1) * tokens, tokens)],
-            send_sem=relay_send.at[index],
-            recv_sem=act_recv.at[index + 1],
-            device_id=peer((0, 0, 1)),
-            device_id_type=MESH,
-        )
-        relay.start()
-        sends.append(relay)
-    own_act.wait()
-    for index, offset in enumerate(slots):
-        if offset[2] != 0:
-            act_in[index].wait_recv()
-
-    parts = []
-    for k in range(levels):
-        own_cots[k].wait()
-        for index in range(1, len(slots)):
-            cot_in[k, index].wait_recv()
-        part = lax.dot_general(
-            cots[k], acts[...], (((0,), (0,)), ((), ())), preferred_element_type=jnp.float32
-        )
-        if k < levels - 1:
-            outgoing[k] = part.astype(jnp.bfloat16)
+        for other in range(part * levels, turn):
+            parts[other].wait_recv()
+            term += incoming[other].astype(jnp.float32)
+        start = here * piece + part * part_rows
+        mine = pl.ds(pl.multiple_of(start, part_rows), part_rows)
+        grad[mine] = term.astype(jnp.bfloat16)
+        for step in range(1, copies):
             copy = pltpu.make_async_remote_copy(
-                src_ref=outgoing.at[k],
-                dst_ref=incoming.at[k],
-                send_sem=part_send.at[k],
-                recv_sem=part_recv.at[k],
-                device_id=level_peer(k + 1),
+                src_ref=grad.at[mine],
+                dst_ref=grad.at[mine],
+                send_sem=grad_send.at[part, step],
+                recv_sem=grad_recv.at[part, step],
+                device_id=((here + step) % copies, shard),
                 device_id_type=MESH,
             )
             copy.start()
-            parts.append(copy)
-    total = part
-    for k in range(levels - 1):
-        parts[k].wait_recv()
-        total += incoming[k].astype(jnp.float32)
-    mine = pl.ds(pl.multiple_of(here * piece, piece), piece)
-    grad[mine] = total.astype(jnp.bfloat16)
-    finals = []
-    for step in range(1, copies):
-        copy = pltpu.make_async_remote_copy(
-            src_ref=grad.at[mine],
-            dst_ref=grad.at[mine],
-            send_sem=grad_send.at[step],
-            recv_sem=grad_recv.at[step],
-            device_id=((here + step) % copies, shard),
-            device_id_type=MESH,
-        )
-        copy.start()
-        finals.append(copy)
-    for copy in sends + parts:
+            finals.append(copy)
+    for copy in sends:
         copy.wait_send()
     for copy in finals:
         copy.wait()
@@ -301,31 +316,32 @@
     tokens, block = activations.shape
     team = CORES * LANES
     many = copies * team
-    piece = rows // copies
+    turns = SPLIT * levels
+    part_rows = rows // copies // SPLIT
     dma = pltpu.SemaphoreType.DMA
     return pl.pallas_call(
-        functools.partial(exchange_kernel, (copies, levels, block, tokens, rows)),
+        functools.partial(exchange_kernel, (copies, levels, tokens, rows)),
         out_shape=jax.ShapeDtypeStruct((rows, block), jnp.bfloat16),
-        in_specs=[pl.BlockSpec(memory_space=pl.ANY), pl.BlockSpec(memory_space=pl.ANY)],
+        in_specs=[pl.BlockSpec(memory_space=pltpu.HBM)] * 2,
         out_specs=pl.BlockSpec(memory_space=pltpu.VMEM),
         scratch_shapes=[
-            pltpu.VMEM((levels, many * tokens, piece), jnp.bfloat16),
+            pltpu.VMEM((turns, many * tokens, part_rows), jnp.bfloat16),
             pltpu.VMEM((many * tokens, block), jnp.bfloat16),
-            pltpu.VMEM((levels, piece, block), jnp.bfloat16),
-            pltpu.VMEM((levels, piece, block), jnp.bfloat16),
+            pltpu.VMEM((turns, part_rows, block), jnp.bfloat16),
+            pltpu.VMEM((turns, part_rows, block), jnp.bfloat16),
             pltpu.VMEM((rows, block), jnp.bfloat16),
-            dma((1 + levels,)),
+            dma((1 + turns,)),
             dma((many,)),
             dma((many,)),
             dma((many,)),
-            dma((levels, many)),
-            dma((levels, many)),
-            dma((levels,)),
-            dma((levels,)),
-            dma((copies,)),
-            dma((copies,)),
+            dma((turns, many)),
+            dma((turns, many)),
+            dma((turns,)),
+            dma((turns,)),
+            dma((SPLIT, copies)),
+            dma((SPLIT, copies)),
         ],
-        compiler_params=pltpu.CompilerParams(collective_id=0, has_side_effects=True),
+        compiler_params=pltpu.CompilerParams(collective_id=0, has_side_effects=True, vmem_limit_bytes=VMEM),
         name="exchange",
     )(cotangents, activations)
 
@@ -347,7 +363,17 @@
 
 
 def refresh_kernel(grad_ref, stats_ref, roots_ref, ages_ref, fresh_ref,
-                   update_ref, new_stats_ref, new_roots_ref):
+                   update_out, new_stats_out, new_roots_out,
+                   update_ref, new_stats_ref, new_roots_ref, old_roots_ref, sem):
+    old_roots = pltpu.make_async_copy(roots_ref, old_roots_ref, sem.at[5])
+    old_roots.start()
+    pending = []
+
+    def put(source, target):
+        copy = pltpu.make_async_copy(source, target, sem.at[len(pending)])
+        copy.start()
+        pending.append(copy)
+
     first = 2 * lax.axis_index("shard")
     block = grad_ref.shape[0]
     grad = grad_ref[...]
@@ -360,6 +386,7 @@
         old = stats_ref[side]
         new = jnp.where(is_fresh, decay * old + (1.0 - decay) * grams[side](), old)
         new_stats_ref[side] = new
+        put(new_stats_ref.at[side], new_stats_out.at[side])
         total = jnp.sum(jnp.sum(new * new, axis=0, keepdims=True), axis=1, keepdims=True)
         scaling = 2.5 / jnp.sqrt(total + tiny_term)
         maps.append((0.25 * scaling) * new)
@@ -373,20 +400,26 @@
     column = lax.broadcasted_iota(jnp.int32, (block, block), 1)
     diagonal = jnp.where(row == column, 1.25**3, 0.0)
     roots = []
+    old_roots.wait()
     for side in range(2):
         last = diagonal + 1.25 * x2[side] - 1.5625 * n3[side]
         last = last - product(small(x2[side]), small(n3[side]))
         root = small(scales[side] * last)
-        root = jnp.where(fresh[side], root, roots_ref[side])
+        root = jnp.where(fresh[side], root, old_roots_ref[side])
         new_roots_ref[side] = root
+        put(new_roots_ref.at[side], new_roots_out.at[side])
         roots.append(root)
     mixed = small(product(grad, roots[1]))
     update_ref[...] = small(product(roots[0], mixed) * math.sqrt(block))
+    put(update_ref, update_out)
+    for copy in pending:
+        copy.wait()
 
 
 def refresh_roots(gradient, statistics, roots, ages, refresh):
     vmem = pl.BlockSpec(memory_space=pltpu.VMEM)
     smem = pl.BlockSpec(memory_space=pltpu.SMEM)
+    hbm = pl.BlockSpec(memory_space=pltpu.HBM)
     return pl.pallas_call(
         refresh_kernel,
         out_shape=(
@@ -394,8 +427,16 @@
             jax.ShapeDtypeStruct(statistics.shape, jnp.float32),
             jax.ShapeDtypeStruct(roots.shape, jnp.bfloat16),
         ),
-        in_specs=[vmem, vmem, vmem, smem, smem],
-        out_specs=(vmem, vmem, vmem),
+        in_specs=[vmem, vmem, hbm, smem, smem],
+        out_specs=(hbm,) * 3,
+        scratch_shapes=[
+            pltpu.VMEM(gradient.shape, jnp.bfloat16),
+            pltpu.VMEM(statistics.shape, jnp.float32),
+            pltpu.VMEM(roots.shape, jnp.bfloat16),
+            pltpu.VMEM(roots.shape, jnp.bfloat16),
+            pltpu.SemaphoreType.DMA((6,)),
+        ],
+        compiler_params=pltpu.CompilerParams(vmem_limit_bytes=VMEM),
         name="refresh_roots",
     )(gradient, statistics, roots, ages, refresh)
 
@@ -406,7 +447,7 @@
     rows = statistics.shape[1]
     block = activations.shape[1]
     team = CORES * LANES
-    if rows != block or shards % team or rows % copies or (rows // copies) % 128:
+    if rows != block or shards % team or rows % copies or (rows // copies) % (128 * SPLIT):
         return general(activations, cotangents, statistics, roots, ages, refresh)
     gradient = exchange(cotangents, activations, copies, shards // team, rows)
     return refresh_roots(gradient, statistics, roots, ages, refresh)

time: 63.3 us -> 63.4 us (level)
  the two profiles are of different devices: /device:TPU:0 before, /device:TPU:10 now
where the time goes in v2:
time: 63.4 us; the launch traced here: 63.2 us
  Pallas kernels  58.8 us (93%)
  local copies, waits for them, and re-layouts  3.72 us (6%)
  between operations  0.68 us (1%)
    pallas_call x1, Pallas kernels, exchange(): pl.pallas_call(functools.partial(exchange_kernel, (copies, levels, tokens...  50.5 us
    pallas_call x1, Pallas kernels, refresh_roots(): pl.pallas_call(refresh_kernel, out_shape=(jax.ShapeDtypeStruct(gradient.s...  8.31 us
    unnamed x12, local copies, waits for them, and re-layouts  3.72 us

profile of v2, /device:TPU:10, one launch (start us, length us, event | category | flops | bytes accessed | tf_op | source)
XLA Modules:
  0.0 63.2 jit_solution(10533695223400312339)
XLA Ops:
  0.6 0.0 copy-start
  0.6 1.6 %copy-done = bf16[128,8192]{1,0:T(8,128)(2,1)S(1)} copy-done((bf16[128,8192]{1,0:T(8,128)(2,1)S(1)}, bf16[128,8192]{1,0:T(8,128)(2,1)}, u32[]{:S(2)}) %copy-start) | copy-done | bytes 2097176
  2.2 0.0 copy-start.3
  2.2 0.9 %copy-done.3 = bf16[128,512]{1,0:T(8,128)(2,1)S(1)} copy-done((bf16[128,512]{1,0:T(8,128)(2,1)S(1)}, bf16[128,512]{1,0:T(8,128)(2,1)}, u32[]{:S(2)}) %copy-start.3) | copy-done | bytes 131096
  3.1 0.0 copy-start.1
  3.1 0.0 copy-start.4
  3.1 0.0 copy-start.5
  3.1 50.5 %exchange.1.grad_ref = bf16[512,512]{1,0:T(8,128)(2,1)S(1)} custom-call(bf16[128,8192]{1,0:T(8,128)(2,1)S(1)} %copy-done, bf16[128,512]{1,0:T(8,128)(2,1)S(1)} %copy-done.3), custom_call_target="tpu_custom_call" | custom-call | tf_op jit(solution)/shard_map/exchange/pallas_call | solution.py:322
  53.6 0.0 copy-done.1
  53.7 0.0 copy-done.4
  53.7 0.0 copy-done.5
  53.7 0.0 copy-start.2
  53.7 1.2 %copy-done.2 = bf16[2,512,512]{2,1,0:T(8,128)(2,1)S(1)} copy-done((bf16[2,512,512]{2,1,0:T(8,128)(2,1)S(1)}, bf16[2,512,512]{2,1,0:T(8,128)(2,1)}, u32[]{:S(2)}) %copy-start.2) | copy-done | bytes 1048600
  54.9 8.3 %refresh_roots.1 = (bf16[512,512]{1,0:T(8,128)(2,1)}, f32[2,512,512]{2,1,0:T(8,128)}, bf16[2,512,512]{2,1,0:T(8,128)(2,1)}) custom-call(bf16[512,512]{1,0:T(8,128)(2,1)S(1)} %exchange.1.grad_ref, f32[2,512,512]{2,1,0:T(8,128)S(1)} %copy-done.1, bf16[2,512,512]{2,1,0:T(8,128)(2,1)S(1)} %copy-done.2, s32[32]{0:T(128)S(1)} %copy-done.4, s32[32]{0:T(128)S(1)} %copy-done.5), custom_call_target="tpu_custom_call" | custom-call | tf_op jit(solution)/shard_map/refresh_roots/pallas_call | solution.py:423
Async XLA Ops:
  0.6 1.6 %copy-start = (bf16[128,8192]{1,0:T(8,128)(2,1)S(1)}, bf16[128,8192]{1,0:T(8,128)(2,1)}, u32[]{:S(2)}) copy-start(bf16[128,8192]{1,0:T(8,128)(2,1)} %cot_ref.1) | copy-start | bytes 6291460
  2.2 0.9 %copy-start.3 = (bf16[128,512]{1,0:T(8,128)(2,1)S(1)}, bf16[128,512]{1,0:T(8,128)(2,1)}, u32[]{:S(2)}) copy-start(bf16[128,512]{1,0:T(8,128)(2,1)} %act_ref.1) | copy-start | bytes 393220
  3.1 50.5 %copy-start.1 = (f32[2,512,512]{2,1,0:T(8,128)S(1)}, f32[2,512,512]{2,1,0:T(8,128)}, u32[]{:S(2)}) copy-start(f32[2,512,512]{2,1,0:T(8,128)} %stats_ref.1) | copy-start | bytes 6291460
  3.1 50.5 %copy-start.4 = (s32[32]{0:T(128)S(1)}, s32[32]{0:T(128)}, u32[]{:S(2)}) copy-start(s32[32]{0:T(128)} %ages_ref.1) | copy-start | bytes 388
  3.1 50.5 %copy-start.5 = (s32[32]{0:T(128)S(1)}, s32[32]{0:T(128)}, u32[]{:S(2)}) copy-start(s32[32]{0:T(128)} %fresh_ref.1) | copy-start | bytes 388
  53.7 1.2 %copy-start.2 = (bf16[2,512,512]{2,1,0:T(8,128)(2,1)S(1)}, bf16[2,512,512]{2,1,0:T(8,128)(2,1)}, u32[]{:S(2)}) copy-start(bf16[2,512,512]{2,1,0:T(8,128)(2,1)} %roots_ref.1) | copy-start | bytes 3145732

commit v3 on v2

--- a/solution.py
+++ b/solution.py
@@ -150,8 +150,8 @@
 
 CORES = 2
 LANES = 2
+LEVELS = 4
 SPLIT = 2
-VMEM = 24 << 20
 MESH = pl.DeviceIdType.MESH
 
 
@@ -170,18 +170,22 @@
     lane = (shard // CORES) % LANES
     core = shard % CORES
     slots = [(a, b, c) for a in range(copies) for b in range(LANES) for c in range(CORES)]
-    steps = [(part, k) for part in range(SPLIT) for k in range(levels)]
+    steps = [(part, k) for k in range(levels) for part in range(SPLIT)]
 
     def peer(offset):
         a, b, c = offset
         other = (level * LANES + (lane + b) % LANES) * CORES + (core + c) % CORES
         return ((here + a) % copies, other)
 
-    def level_peer(step):
-        return (here, ((level + step) % levels) * team + lane * CORES + core)
+    beside = level + 1 - 2 * (level % 2)
+    targets = [(beside + 2) % levels, (level + 2) % levels, beside, level]
+    receivers = [beside, (level + 2) % levels, beside]
+
+    def level_peer(other):
+        return (here, other * team + lane * CORES + core)
 
     def columns(device, part, k):
-        target = ((level + k + 1) % levels) * team + device[1] % team
+        target = targets[k] * team + device[1] % team
         start = target * rows + device[0] * piece + part * part_rows
         return pl.ds(pl.multiple_of(start, part_rows), part_rows)
 
@@ -191,8 +195,8 @@
     barrier = pltpu.get_barrier_semaphore()
     for offset in slots[1:]:
         pl.semaphore_signal(barrier, inc=1, device_id=peer(offset), device_id_type=MESH)
-    for step in range(1, levels):
-        pl.semaphore_signal(barrier, inc=1, device_id=level_peer(step), device_id_type=MESH)
+    for other in receivers[:2]:
+        pl.semaphore_signal(barrier, inc=1, device_id=level_peer(other), device_id_type=MESH)
     own_act = pltpu.make_async_copy(act_ref, acts.at[token_rows(0)], local_sem.at[0])
     own_act.start()
     own_cots = []
@@ -204,7 +208,7 @@
         )
         own.start()
         own_cots.append(own)
-    pl.semaphore_wait(barrier, len(slots) - 1 + levels - 1)
+    pl.semaphore_wait(barrier, len(slots) - 1 + 2)
 
     sends = []
 
@@ -242,25 +246,15 @@
                 cot_in[turn, index] = copy
 
     act_in = {}
-    for a in range(1, copies):
-        act_in[a, 0, 0] = send_act((a, 0, 0), True, (a, 0, 0))
-    for b in range(1, LANES):
-        act_in[0, b, 0] = send_act((0, b, 0), True, (0, b, 0))
-    for c in range(1, CORES):
-        act_in[0, 0, c] = send_act((0, 0, c), True, (0, 0, c))
-    send_cots(range(1))
-    for a in range(1, copies):
-        act_in[a, 0, 0].wait_recv()
-        for b in range(1, LANES):
-            act_in[a, b, 0] = send_act((a, b, 0), False, (0, b, 0))
-    send_cots(range(1, len(steps)))
-    for a in range(copies):
-        for b in range(LANES):
-            if b:
+    for offset in slots[1:]:
+        if not offset[2] or offset[:2] == (0, 0):
+            act_in[offset] = send_act(offset, True, offset)
+    send_cots(range(len(steps)))
+    for a, b, c in slots[1:]:
+        if c and (a or b):
+            if c == 1:
                 act_in[a, b, 0].wait_recv()
-            if a or b:
-                for c in range(1, CORES):
-                    act_in[a, b, c] = send_act((a, b, c), False, (0, 0, c))
+            act_in[a, b, c] = send_act((a, b, c), False, (0, 0, c))
     own_act.wait()
     for offset in slots:
         if offset[2]:
@@ -274,6 +268,9 @@
         term = lax.dot_general(
             cots[turn], acts[...], (((0,), (0,)), ((), ())), preferred_element_type=jnp.float32
         )
+        if k == 1:
+            parts[part, 0].wait_recv()
+            term += incoming[part].astype(jnp.float32)
         if k < levels - 1:
             outgoing[turn] = term.astype(jnp.bfloat16)
             copy = pltpu.make_async_remote_copy(
@@ -281,16 +278,16 @@
                 dst_ref=incoming.at[turn],
                 send_sem=part_send.at[turn],
                 recv_sem=part_recv.at[turn],
-                device_id=level_peer(k + 1),
+                device_id=level_peer(receivers[k]),
                 device_id_type=MESH,
             )
             copy.start()
             sends.append(copy)
-            parts[turn] = copy
+            parts[part, k] = copy
             continue
-        for other in range(part * levels, turn):
-            parts[other].wait_recv()
-            term += incoming[other].astype(jnp.float32)
+        for other in range(1, k):
+            parts[part, other].wait_recv()
+            term += incoming[other * SPLIT + part].astype(jnp.float32)
         start = here * piece + part * part_rows
         mine = pl.ds(pl.multiple_of(start, part_rows), part_rows)
         grad[mine] = term.astype(jnp.bfloat16)
@@ -341,7 +338,7 @@
             dma((SPLIT, copies)),
             dma((SPLIT, copies)),
         ],
-        compiler_params=pltpu.CompilerParams(collective_id=0, has_side_effects=True, vmem_limit_bytes=VMEM),
+        compiler_params=pltpu.CompilerParams(collective_id=0, has_side_effects=True),
         name="exchange",
     )(cotangents, activations)
 
@@ -364,8 +361,13 @@
 
 def refresh_kernel(grad_ref, stats_ref, roots_ref, ages_ref, fresh_ref,
                    update_out, new_stats_out, new_roots_out,
-                   update_ref, new_stats_ref, new_roots_ref, old_roots_ref, sem):
+                   update_ref, new_stats_ref, new_roots_ref, old_stats_ref, old_roots_ref, sem):
     old_roots = pltpu.make_async_copy(roots_ref, old_roots_ref, sem.at[5])
+    old_stats = []
+    for side in range(2):
+        load = pltpu.make_async_copy(stats_ref.at[side], old_stats_ref.at[side], sem.at[6 + side])
+        load.start()
+        old_stats.append(load)
     old_roots.start()
     pending = []
 
@@ -383,8 +385,10 @@
         is_fresh = fresh_ref[first + side] == 1
         age = jnp.full((1, 1), ages_ref[first + side].astype(jnp.float32), jnp.float32)
         decay = jnp.exp(age * math.log(decay_base))
-        old = stats_ref[side]
-        new = jnp.where(is_fresh, decay * old + (1.0 - decay) * grams[side](), old)
+        gram = grams[side]()
+        old_stats[side].wait()
+        old = old_stats_ref[side]
+        new = jnp.where(is_fresh, decay * old + (1.0 - decay) * gram, old)
         new_stats_ref[side] = new
         put(new_stats_ref.at[side], new_stats_out.at[side])
         total = jnp.sum(jnp.sum(new * new, axis=0, keepdims=True), axis=1, keepdims=True)
@@ -427,16 +431,16 @@
             jax.ShapeDtypeStruct(statistics.shape, jnp.float32),
             jax.ShapeDtypeStruct(roots.shape, jnp.bfloat16),
         ),
-        in_specs=[vmem, vmem, hbm, smem, smem],
+        in_specs=[vmem, hbm, hbm, smem, smem],
         out_specs=(hbm,) * 3,
         scratch_shapes=[
             pltpu.VMEM(gradient.shape, jnp.bfloat16),
             pltpu.VMEM(statistics.shape, jnp.float32),
             pltpu.VMEM(roots.shape, jnp.bfloat16),
+            pltpu.VMEM(statistics.shape, jnp.float32),
             pltpu.VMEM(roots.shape, jnp.bfloat16),
-            pltpu.SemaphoreType.DMA((6,)),
+            pltpu.SemaphoreType.DMA((8,)),
         ],
-        compiler_params=pltpu.CompilerParams(vmem_limit_bytes=VMEM),
         name="refresh_roots",
     )(gradient, statistics, roots, ages, refresh)
 
@@ -447,7 +451,7 @@
     rows = statistics.shape[1]
     block = activations.shape[1]
     team = CORES * LANES
-    if rows != block or shards % team or rows % copies or (rows // copies) % (128 * SPLIT):
+    if rows != block or shards != LEVELS * team or rows % copies or (rows // copies) % (128 * SPLIT):
         return general(activations, cotangents, statistics, roots, ages, refresh)
     gradient = exchange(cotangents, activations, copies, shards // team, rows)
     return refresh_roots(gradient, statistics, roots, ages, refresh)

time: 63.4 us -> 59.2 us (0.934)
  the two profiles are of different devices: /device:TPU:10 before, /device:TPU:0 now
where the time goes in v3:
time: 59.2 us; the launch traced here: 59 us
  Pallas kernels  58.4 us (99%)
  between operations  0.64 us (1%)
    pallas_call x1, Pallas kernels, exchange(): pl.pallas_call(functools.partial(exchange_kernel, (copies, levels, tokens...  48 us
    pallas_call x1, Pallas kernels, refresh_roots(): pl.pallas_call(refresh_kernel, out_shape=(jax.ShapeDtypeStruct(gradient.s...  10.3 us

profile of v3, /device:TPU:0, one launch (start us, length us, event | category | flops | bytes accessed | tf_op | source)
XLA Modules:
  0.0 59.0 jit_solution(8135387521516471540)
XLA Ops:
  0.6 48.0 %exchange.1.grad_ref = bf16[512,512]{1,0:T(8,128)(2,1)} custom-call(bf16[128,8192]{1,0:T(8,128)(2,1)} %cot_ref.1, bf16[128,512]{1,0:T(8,128)(2,1)} %act_ref.1), custom_call_target="tpu_custom_call" | custom-call | tf_op jit(solution)/shard_map/exchange/pallas_call | solution.py:319
  48.7 10.3 %refresh_roots.1 = (bf16[512,512]{1,0:T(8,128)(2,1)}, f32[2,512,512]{2,1,0:T(8,128)}, bf16[2,512,512]{2,1,0:T(8,128)(2,1)}) custom-call(bf16[512,512]{1,0:T(8,128)(2,1)} %exchange.1.grad_ref, f32[2,512,512]{2,1,0:T(8,128)} %stats_ref.1, bf16[2,512,512]{2,1,0:T(8,128)(2,1)} %roots_ref.1, s32[32]{0:T(128)} %ages_ref.1, s32[32]{0:T(128)} %fresh_ref.1), custom_call_target="tpu_custom_call" | custom-call | tf_op jit(solution)/shard_map/refresh_roots/pallas_call | solution.py:427

commit v4 on v3

--- a/solution.py
+++ b/solution.py
@@ -151,7 +151,9 @@
 CORES = 2
 LANES = 2
 LEVELS = 4
+VMEM = 24 << 20
 SPLIT = 2
+AHEAD = 3
 MESH = pl.DeviceIdType.MESH
 
 
@@ -249,7 +251,7 @@
     for offset in slots[1:]:
         if not offset[2] or offset[:2] == (0, 0):
             act_in[offset] = send_act(offset, True, offset)
-    send_cots(range(len(steps)))
+    send_cots(range(AHEAD))
     for a, b, c in slots[1:]:
         if c and (a or b):
             if c == 1:
@@ -284,6 +286,7 @@
             copy.start()
             sends.append(copy)
             parts[part, k] = copy
+            send_cots(range(turn + AHEAD, min(turn + AHEAD + 1, len(steps))))
             continue
         for other in range(1, k):
             parts[part, other].wait_recv()
@@ -307,6 +310,10 @@
     for copy in finals:
         copy.wait()
     grad_ref[...] = grad[...]
+
+
+def pinned(x):
+    return pltpu.with_memory_space_constraint(x, pltpu.HBM)
 
 
 def exchange(cotangents, activations, copies, levels, rows):
@@ -338,9 +345,9 @@
             dma((SPLIT, copies)),
             dma((SPLIT, copies)),
         ],
-        compiler_params=pltpu.CompilerParams(collective_id=0, has_side_effects=True),
+        compiler_params=pltpu.CompilerParams(collective_id=0, has_side_effects=True, vmem_limit_bytes=VMEM),
         name="exchange",
-    )(cotangents, activations)
+    )(pinned(cotangents), pinned(activations))
 
 
 def product(left, right, contract=((1,), (0,))):
@@ -361,13 +368,8 @@
 
 def refresh_kernel(grad_ref, stats_ref, roots_ref, ages_ref, fresh_ref,
                    update_out, new_stats_out, new_roots_out,
-                   update_ref, new_stats_ref, new_roots_ref, old_stats_ref, old_roots_ref, sem):
+                   update_ref, new_stats_ref, new_roots_ref, old_roots_ref, sem):
     old_roots = pltpu.make_async_copy(roots_ref, old_roots_ref, sem.at[5])
-    old_stats = []
-    for side in range(2):
-        load = pltpu.make_async_copy(stats_ref.at[side], old_stats_ref.at[side], sem.at[6 + side])
-        load.start()
-        old_stats.append(load)
     old_roots.start()
     pending = []
 
@@ -386,8 +388,7 @@
         age = jnp.full((1, 1), ages_ref[first + side].astype(jnp.float32), jnp.float32)
         decay = jnp.exp(age * math.log(decay_base))
         gram = grams[side]()
-        old_stats[side].wait()
-        old = old_stats_ref[side]
+        old = stats_ref[side]
         new = jnp.where(is_fresh, decay * old + (1.0 - decay) * gram, old)
         new_stats_ref[side] = new
         put(new_stats_ref.at[side], new_stats_out.at[side])
@@ -431,18 +432,18 @@
             jax.ShapeDtypeStruct(statistics.shape, jnp.float32),
             jax.ShapeDtypeStruct(roots.shape, jnp.bfloat16),
         ),
-        in_specs=[vmem, hbm, hbm, smem, smem],
+        in_specs=[vmem, vmem, hbm, smem, smem],
         out_specs=(hbm,) * 3,
         scratch_shapes=[
             pltpu.VMEM(gradient.shape, jnp.bfloat16),
             pltpu.VMEM(statistics.shape, jnp.float32),
             pltpu.VMEM(roots.shape, jnp.bfloat16),
-            pltpu.VMEM(statistics.shape, jnp.float32),
             pltpu.VMEM(roots.shape, jnp.bfloat16),
-            pltpu.SemaphoreType.DMA((8,)),
+            pltpu.SemaphoreType.DMA((6,)),
         ],
+        compiler_params=pltpu.CompilerParams(vmem_limit_bytes=VMEM),
         name="refresh_roots",
-    )(gradient, statistics, roots, ages, refresh)
+    )(gradient, statistics, pinned(roots), ages, refresh)
 
 
 def per_device(activations, cotangents, statistics, roots, ages, refresh):

time: 59.2 us -> 56.3 us (0.951)
  Pallas kernels: 58.4 us -> 55.4 us
    pallas_call x1, Pallas kernels: 10.3 us -> 8.23 us  [refresh_roots(): pl.pallas_call(refresh_kernel, out_shape=(jax.ShapeDtypeStruct(gradient.s...]
    pallas_call x1, Pallas kernels: 48 us -> 47.2 us  [exchange(): pl.pallas_call(functools.partial(exchange_kernel, (copies, levels, tokens...]
where the time goes in v4:
time: 56.3 us; the launch traced here: 56.1 us
  Pallas kernels  55.4 us (98%)
  between operations  0.69 us (1%)
    pallas_call x1, Pallas kernels, exchange(): pl.pallas_call(functools.partial(exchange_kernel, (copies, levels, tokens...  47.2 us
    pallas_call x1, Pallas kernels, refresh_roots(): pl.pallas_call(refresh_kernel, out_shape=(jax.ShapeDtypeStruct(gradient.s...  8.23 us

profile of v4, /device:TPU:0, one launch (start us, length us, event | category | flops | bytes accessed | tf_op | source)
XLA Modules:
  0.0 56.1 jit_solution(10496555723097522875)
XLA Ops:
  0.6 0.0 copy-start.2
  0.6 0.0 copy-start.1
  0.7 0.0 copy-start
  0.7 47.2 %exchange.1.grad_ref = bf16[512,512]{1,0:T(8,128)(2,1)S(1)} custom-call(bf16[128,8192]{1,0:T(8,128)(2,1)} %cot_ref.1, bf16[128,512]{1,0:T(8,128)(2,1)} %act_ref.1), custom_call_target="tpu_custom_call" | custom-call | tf_op jit(solution)/shard_map/exchange/pallas_call | solution.py:326
  47.9 0.0 copy-done.2
  47.9 0.0 copy-done.1
  47.9 0.0 copy-done
  47.9 8.2 %refresh_roots.1 = (bf16[512,512]{1,0:T(8,128)(2,1)}, f32[2,512,512]{2,1,0:T(8,128)}, bf16[2,512,512]{2,1,0:T(8,128)(2,1)}) custom-call(bf16[512,512]{1,0:T(8,128)(2,1)S(1)} %exchange.1.grad_ref, f32[2,512,512]{2,1,0:T(8,128)S(1)} %copy-done, bf16[2,512,512]{2,1,0:T(8,128)(2,1)} %roots_ref.1, s32[32]{0:T(128)S(1)} %copy-done.1, s32[32]{0:T(128)S(1)} %copy-done.2), custom_call_target="tpu_custom_call" | custom-call | tf_op jit(solution)/shard_map/refresh_roots/pallas_call | solution.py:428
Async XLA Ops:
  0.6 47.3 %copy-start.2 = (s32[32]{0:T(128)S(1)}, s32[32]{0:T(128)}, u32[]{:S(2)}) copy-start(s32[32]{0:T(128)} %fresh_ref.1) | copy-start | bytes 388
  0.6 47.3 %copy-start.1 = (s32[32]{0:T(128)S(1)}, s32[32]{0:T(128)}, u32[]{:S(2)}) copy-start(s32[32]{0:T(128)} %ages_ref.1) | copy-start | bytes 388
  0.7 47.3 %copy-start = (f32[2,512,512]{2,1,0:T(8,128)S(1)}, f32[2,512,512]{2,1,0:T(8,128)}, u32[]{:S(2)}) copy-start(f32[2,512,512]{2,1,0:T(8,128)} %stats_ref.1) | copy-start | bytes 6291460

commit v5 on v4

--- a/solution.py
+++ b/solution.py
@@ -172,7 +172,9 @@
     lane = (shard // CORES) % LANES
     core = shard % CORES
     slots = [(a, b, c) for a in range(copies) for b in range(LANES) for c in range(CORES)]
-    steps = [(part, k) for k in range(levels) for part in range(SPLIT)]
+    steps = [(part, 0) for part in range(SPLIT)]
+    steps += [(part, k) for part in range(SPLIT) for k in range(1, levels - 1)]
+    steps += [(part, levels - 1) for part in range(SPLIT)]
 
     def peer(offset):
         a, b, c = offset
@@ -272,7 +274,7 @@
         )
         if k == 1:
             parts[part, 0].wait_recv()
-            term += incoming[part].astype(jnp.float32)
+            term += incoming[steps.index((part, 0))].astype(jnp.float32)
         if k < levels - 1:
             outgoing[turn] = term.astype(jnp.bfloat16)
             copy = pltpu.make_async_remote_copy(
@@ -290,7 +292,7 @@
             continue
         for other in range(1, k):
             parts[part, other].wait_recv()
-            term += incoming[other * SPLIT + part].astype(jnp.float32)
+            term += incoming[steps.index((part, other))].astype(jnp.float32)
         start = here * piece + part * part_rows
         mine = pl.ds(pl.multiple_of(start, part_rows), part_rows)
         grad[mine] = term.astype(jnp.bfloat16)

time: 56.3 us -> 53.5 us (0.950)
  Pallas kernels: 55.4 us -> 52.6 us
    pallas_call x1, Pallas kernels: 47.2 us -> 44.4 us  [exchange(): pl.pallas_call(functools.partial(exchange_kernel, (copies, levels, tokens...]
where the time goes in v5:
time: 53.5 us; the launch traced here: 53.3 us
  Pallas kernels  52.6 us (98%)
  between operations  0.69 us (1%)
    pallas_call x1, Pallas kernels, exchange(): pl.pallas_call(functools.partial(exchange_kernel, (copies, levels, tokens...  44.4 us
    pallas_call x1, Pallas kernels, refresh_roots(): pl.pallas_call(refresh_kernel, out_shape=(jax.ShapeDtypeStruct(gradient.s...  8.22 us

profile of v5, /device:TPU:0, one launch (start us, length us, event | category | flops | bytes accessed | tf_op | source)
XLA Modules:
  0.0 53.3 jit_solution(1351638855170282482)
XLA Ops:
  0.6 0.0 copy-start.2
  0.6 0.0 copy-start.1
  0.7 0.0 copy-start
  0.7 44.4 %exchange.1.grad_ref = bf16[512,512]{1,0:T(8,128)(2,1)S(1)} custom-call(bf16[128,8192]{1,0:T(8,128)(2,1)} %cot_ref.1, bf16[128,512]{1,0:T(8,128)(2,1)} %act_ref.1), custom_call_target="tpu_custom_call" | custom-call | tf_op jit(solution)/shard_map/exchange/pallas_call | solution.py:328
  45.1 0.0 copy-done.2
  45.1 0.0 copy-done.1
  45.1 0.0 copy-done
  45.1 8.2 %refresh_roots.1 = (bf16[512,512]{1,0:T(8,128)(2,1)}, f32[2,512,512]{2,1,0:T(8,128)}, bf16[2,512,512]{2,1,0:T(8,128)(2,1)}) custom-call(bf16[512,512]{1,0:T(8,128)(2,1)S(1)} %exchange.1.grad_ref, f32[2,512,512]{2,1,0:T(8,128)S(1)} %copy-done, bf16[2,512,512]{2,1,0:T(8,128)(2,1)} %roots_ref.1, s32[32]{0:T(128)S(1)} %copy-done.1, s32[32]{0:T(128)S(1)} %copy-done.2), custom_call_target="tpu_custom_call" | custom-call | tf_op jit(solution)/shard_map/refresh_roots/pallas_call | solution.py:430
Async XLA Ops:
  0.6 44.4 %copy-start.2 = (s32[32]{0:T(128)S(1)}, s32[32]{0:T(128)}, u32[]{:S(2)}) copy-start(s32[32]{0:T(128)} %fresh_ref.1) | copy-start | bytes 388
  0.6 44.4 %copy-start.1 = (s32[32]{0:T(128)S(1)}, s32[32]{0:T(128)}, u32[]{:S(2)}) copy-start(s32[32]{0:T(128)} %ages_ref.1) | copy-start | bytes 388
  0.7 44.4 %copy-start = (f32[2,512,512]{2,1,0:T(8,128)S(1)}, f32[2,512,512]{2,1,0:T(8,128)}, u32[]{:S(2)}) copy-start(f32[2,512,512]{2,1,0:T(8,128)} %stats_ref.1) | copy-start | bytes 6291460
